TPU v7x, 32 devices: a whole 2x2x4 slice. The times are simulated.
32 devices in a mesh: req: 8 (over y, x, core), mp: 4 (over z).
Axes of the slice: x: 2, y: 2, z: 4, core: 2. Of those that a mesh axis runs over, the one named last changes fastest.
Arguments:
- latents: bfloat16 [16, 1, 384, 416], P('req', None, 'mp'), may hold values from -12 to 12
- prior_frame_cache: bfloat16 [16, 2, 384, 416], P('req', None, 'mp'), may hold values from -6 to 6
- move_to: int32 [16], P('req'), may hold values from 0 to 15, as said below
- counts: int32 [8], P('req'), may hold values from 1 to 2, as said below
- norm_gain: bfloat16 [384], P('mp'), may hold values from 0.5 to 1.5
- conv_weight: bfloat16 [27, 384, 384], P(None, 'mp'), may hold values from -0.0625 to 0.0625
- conv_bias: float32 [384], P('mp'), may hold values from -1.5 to 1.5
Outputs:
- decoded: bfloat16 [16, 1, 384, 416], P('req', None, 'mp')
- new_cache: bfloat16 [16, 2, 384, 416], P('req', None, 'mp')
Inputs may be any that keep to these rules, and one draw needn't show every extreme that they name: move_to is a permutation of the slots; a stream's new slot lies on its old index of req or on the next or previous one, the last and first index being neighbours; every index hands exactly 1 stream to each neighbour and takes the same number back from it. `counts`: some index of req is full and some other holds a single stream.
All inputs are finite; a program needn't handle non-finite values.
Results may differ from a plain program's by a relative error of at most 0.0018.
Values may be sent and summed in bfloat16 or wider, within the bound.
A program may use at most 64 MiB of HBM per device.

v0:
```python
import jax
import jax.numpy as jnp
from jax import lax
from jax.sharding import PartitionSpec as P

SECTION_CHANNELS = 384
LATENT_COLUMNS = 104


def shifted_2(block, axis, distance):
    devices = range(lax.axis_size(axis))
    route = [((i - distance) % len(devices), i) for i in devices]
    return lax.ppermute(block, axis, route)


def apply_taps(running, shard_in, weights, row_width):
    frames = shard_in.shape[1] - 2
    pixels = shard_in.shape[3]
    padded = jnp.pad(shard_in, ((0, 0), (0, 0), (0, 0), (row_width + 1, row_width + 1)))
    column = jnp.arange(pixels + 2 * row_width) % row_width
    for step_x in range(3):
        inside = ((column + step_x - 1 >= 0) & (column + step_x - 1 < row_width)).astype(
            shard_in.dtype
        )
        shifted = padded[:, :, :, step_x : step_x + pixels + 2 * row_width] * inside
        for step_y in range(3):
            window = shifted[:, :, :, step_y * row_width : step_y * row_width + pixels]
            for step_t in range(3):
                running = running + jnp.einsum(
                    "oc,stcp->stop",
                    weights[step_t * 9 + step_y * 3 + step_x],
                    window[:, step_t : step_t + frames],
                    preferred_element_type=jnp.float32,
                )
    return running


def pack_slots(prior_frame_cache, chosen, target, capacity):
    ranking = jnp.cumsum(chosen.astype(jnp.int32)) - 1
    picker = (chosen[None, :] & (ranking[None, :] == jnp.arange(capacity)[:, None])).astype(
        jnp.bfloat16
    )
    blocks = jnp.einsum(
        "cs,sfkp->cfkp", picker, prior_frame_cache, preferred_element_type=jnp.float32
    ).astype(jnp.bfloat16)
    labels = (jnp.dot(picker.astype(jnp.float32), (target + 1).astype(jnp.float32)) - 1.0).astype(
        jnp.bfloat16
    )
    return (blocks, labels)


def migrate(prior_frame_cache, move_to):
    slot_count = prior_frame_cache.shape[0]
    member_slots = lax.axis_size("req")
    position = lax.axis_index("req")
    capacity = slot_count // 2
    device = move_to // slot_count
    target = move_to % slot_count
    offset = (device - position) % member_slots
    goes_right = offset == 1
    goes_left = offset == member_slots - 1
    stays_put = offset == 0
    blocks_right, labels_right = pack_slots(prior_frame_cache, goes_right, target, capacity)
    blocks_left, labels_left = pack_slots(prior_frame_cache, goes_left, target, capacity)
    from_left = shifted_2((blocks_right, labels_right), "req", 1)
    from_right = shifted_2((blocks_left, labels_left), "req", -1)
    sources = jnp.concatenate([prior_frame_cache, from_left[0], from_right[0]], axis=0)
    own_labels = jnp.where(stays_put, target, -1).astype(jnp.float32)
    labels = jnp.concatenate(
        [own_labels, from_left[1].astype(jnp.float32), from_right[1].astype(jnp.float32)]
    )
    placing = (labels[None, :] == jnp.arange(slot_count, dtype=jnp.float32)[:, None]).astype(
        jnp.bfloat16
    )
    return jnp.einsum("ns,sfkp->nfkp", placing, sources, preferred_element_type=jnp.float32).astype(
        jnp.bfloat16
    )


def normalize(values, squares, gains):
    scaled = (
        values.astype(jnp.float32)
        * lax.rsqrt(squares / SECTION_CHANNELS + 1e-06)
        * gains.astype(jnp.float32)[:, None]
    )
    return jax.nn.silu(scaled).astype(jnp.bfloat16)


def shards(latents, prior_frame_cache, move_to, counts, norm_gain, conv_weight, conv_bias):
    moved = migrate(prior_frame_cache, move_to)
    slot_count = latents.shape[0]
    frames = latents.shape[1]
    live = (jnp.arange(slot_count) < counts[0])[:, None, None, None]
    start_zero = jnp.zeros(
        (slot_count, frames, conv_weight.shape[1], latents.shape[3]), jnp.float32
    )
    values = latents.astype(jnp.float32)
    partial_squares = jnp.sum(values * values, axis=2, keepdims=True)
    squares = lax.psum(partial_squares, "mp")
    hidden = normalize(latents, squares, norm_gain)
    extended = jnp.concatenate([moved, hidden], axis=1)
    conv_sum = apply_taps(
        start_zero, lax.all_gather(extended, "mp", axis=2, tiled=True), conv_weight, LATENT_COLUMNS
    )
    total = latents.astype(jnp.float32) + conv_sum + conv_bias[:, None]
    decoded = jnp.where(live, total, jnp.zeros_like(total)).astype(jnp.bfloat16)
    new_cache = extended[:, frames:]
    return (decoded, new_cache)


def solution(mesh):
    in_specs = (
        P("req", None, "mp", None),
        P("req", None, "mp", None),
        P("req"),
        P("req"),
        P("mp"),
        P(None, "mp", None),
        P("mp"),
    )
    out_specs = (P("req", None, "mp", None), P("req", None, "mp", None))
    return jax.shard_map(shards, mesh=mesh, in_specs=in_specs, out_specs=out_specs, check_vma=False)
```

profile of v0, /device:TPU:0, one launch (start us, length us, event | category | flops | bytes accessed | tf_op | source)
XLA Modules:
  0.0 157.5 jit_solution(8122907851598073962)
XLA Ops:
  7.2 0.7 fusion.140
  8.3 0.6 select_reduce_fusion.1
  9.5 1.5 collective-permute-start
  11.7 4.0 %collective-permute-start.1 = (bf16[1]{0:T(256)(128)(2,1)}, bf16[1]{0:T(256)(128)(2,1)}, u32[]{:S(2)}, u32[]{:S(2)}) collective-permute-start(bf16[1]{0:T(256)(128)(2,1)} %bitcast.7), channel_id=1, source_target_pairs={{4,0},{8,4},{12,8},{16,12},{20,16},{24,20},{28,24},{0,28},{5,1},{9... | collective-permute-start | bytes 14 | tf_op jit(solution)/shard_map/ppermute | solution.py:13
  15.7 1.4 copy.130
  17.1 0.6 fusion.135
  17.7 0.3 copy.128
  18.1 0.6 fusion.133
  18.7 0.3 copy.129
  19.0 2.7 %collective-permute-start.3 = (bf16[1,2,96,416]{3,0,2,1:T(2,128)(2,1)S(1)}, bf16[1,2,96,416]{3,0,2,1:T(2,128)(2,1)S(1)}, u32[]{:S(2)}, u32[]{:S(2)}) collective-permute-start(bf16[1,2,96,416]{3,0,2,1:T(2,128)(2,1)S(1)} %copy.129), channel_id=1, source_target_pairs={{4,0},{8,4},{12,8},{16,12},{20,16},{24,20},{28,24},{0,28},{5,1},{9... | collective-permute-start | bytes 479240 | tf_op jit(solution)/shard_map/ppermute | solution.py:13
  21.7 12.7 %psum.7 = f32[2,1,1,416]{3,0,2,1:T(2,128)S(1)} all-reduce(f32[2,1,1,416]{3,0,2,1:T(2,128)S(1)} %bitcast.336), channel_id=1, replica_groups=mesh['req'=8,'mp'=4] {'mp'}, use_global_device_ids=true, to_apply=%region_3.4 | all-reduce | flops 832 | bytes 6656 | tf_op jit(solution)/shard_map/psum | solution.py:99
  34.5 0.2 fusion.57
  34.7 0.2 copy.131
  36.3 1.5 convolution_convert_fusion
  37.8 1.7 %pad_maximum_fusion.2 = bf16[2,3,96,416]{3,0,2,1:T(2,128)(2,1)} fusion(bf16[2,1,96,416]{3,0,2,1:T(2,128)(2,1)S(1)} %copy.131, bf16[2,2,96,416]{3,0,2,1:T(2,128)(2,1)S(1)} %convolution_convert_fusion), kind=kLoop, calls=%fused_computation.110 | loop fusion | flops 239616 | bytes 958464 | tf_op jit(solution)/shard_map/concatenate | solution.py:101
  40.2 0.6 fusion.49
  40.8 0.8 copy.160
  41.6 45.3 %all-gather.2.cloned.1.call-done = bf16[2,3,384,416]{3,0,2,1:T(2,128)(2,1)} async-done(((bf16[2,3,96,416]{3,0,2,1:T(2,128)(2,1)}), bf16[2,3,384,416]{3,0,2,1:T(2,128)(2,1)}) %all-gather.2.cloned.1.call-update) | async-done | bytes 1916944 | tf_op jit(solution)/shard_map/all_gather | solution.py:103
  87.0 18.8 %slice_multiply_fusion.2 = (bf16[2,3,384,624]{3,0,2,1:T(2,128)(2,1)S(1)}, bf16[2,3,384,624]{3,0,2,1:T(2,128)(2,1)S(1)}, bf16[2,3,384,624]{3,0,2,1:T(2,128)(2,1)S(1)}) fusion(bf16[624]{0:T(1024)(128)(2,1)S(1)} %fusion.127, bf16[2,3,384,416]{3,0,2,1:T(2,128)(2,1)} %all-gather.2.cloned.1.call-done, bf16[624]{0:T(1024)(128)(2,1)S(1)} %fusion.129, ...), kind=kLoop, calls=%fused_computation.2 | loop fusion | flops 17252352 | bytes 10546848 | tf_op jit(solution)/shard_map/mul | solution.py:25
  105.8 10.7 %slice_bitcast_fusion.18 = (bf16[2,384,416]{2,0,1:T(2,128)(2,1)S(1)}, bf16[2,384,416]{2,0,1:T(2,128)(2,1)S(1)}, bf16[2,384,416]{2,0,1:T(2,128)(2,1)S(1)}, bf16[2...) fusion(bf16[2,3,384,624]{3,0,2,1:T(2,128)(2,1)S(1)} %get-tuple-, ...), kind=kLoop, calls=%fused_computation.66 | loop fusion | bytes 11501568 | tf_op jit(solution)/shard_map/reshape.33
  116.5 0.3 fusion.47
  116.8 25.4 %slice_bitcast_fusion.8 = (bf16[2,384,416]{2,0,1:T(2,128)(2,1)S(1)}, bf16[2,384,416]{2,0,1:T(2,128)(2,1)S(1)}, bf16[2,384,416]{2,0,1:T(2,128)(2,1)S(1)}, bf16[2,...) fusion(bf16[2,3,384,624]{3,0,2,1:T(2,128)(2,1)S(1)} %get-tuple-, ...), kind=kLoop, calls=%fused_computation.56 | loop fusion | bytes 23003136 | tf_op jit(solution)/shard_map/reshape.53
  142.2 0.3 convolution_bitcast_fusion.8
  142.5 0.3 convolution_bitcast_fusion
  142.7 0.3 convolution_bitcast_fusion.1
  143.0 0.3 convolution_bitcast_fusion.2
  143.3 0.3 convolution_bitcast_fusion.3
  143.6 0.3 convolution_bitcast_fusion.4
  143.9 0.3 convolution_bitcast_fusion.5
  144.2 0.3 convolution_bitcast_fusion.6
  144.5 0.3 convolution_bitcast_fusion.7
  144.8 0.3 convolution_bitcast_fusion.9
  145.1 0.3 convolution_add_fusion.14
  145.4 0.3 convolution_add_fusion.13
  145.7 0.3 convolution_add_fusion.12
  145.9 0.3 convolution_add_fusion.11
  146.2 0.3 convolution_add_fusion.10
  146.5 0.3 convolution_add_fusion.9
  146.8 0.3 convolution_add_fusion.8
  147.1 0.3 convolution_add_fusion.7
  147.4 0.3 convolution_add_fusion.6
  147.7 0.3 convolution_add_fusion.5
  148.0 0.3 convolution_add_fusion.4
  148.3 0.3 convolution_add_fusion.3
  148.6 0.3 convolution_add_fusion.2
  148.9 0.3 convolution_add_fusion.1
  149.2 0.3 fusion
  149.6 1.1 fusion.17
  (28 shorter events, 0.8 us)
Async XLA Ops:
  7.2 79.8 %all-gather.2.cloned.1.call-start = ((), (), s32[]{:S(2)}) async-start(), calls=%async_computation | async-start | bytes 2949120 | tf_op jit(solution)/shard_map/all_gather | solution.py:103
  9.5 25.4 %collective-permute-start = (bf16[1]{0:T(256)(128)(2,1)}, bf16[1]{0:T(256)(128)(2,1)}, u32[]{:S(2)}, u32[]{:S(2)}) collective-permute-start(bf16[1]{0:T(256)(128)(2,1)} %bitcast.4), channel_id=1, source_target_pairs={{28,0},{0,4},{4,8},{8,12},{12,16},{16,20},{20,24},{24,28},{29,1},{... | collective-permute-start | bytes 14 | tf_op jit(solution)/shard_map/ppermute | solution.py:13
  11.7 23.9 %collective-permute-start.1 = (bf16[1]{0:T(256)(128)(2,1)}, bf16[1]{0:T(256)(128)(2,1)}, u32[]{:S(2)}, u32[]{:S(2)}) collective-permute-start(bf16[1]{0:T(256)(128)(2,1)} %bitcast.7), channel_id=1, source_target_pairs={{4,0},{8,4},{12,8},{16,12},{20,16},{24,20},{28,24},{0,28},{5,1},{9... | collective-permute-start | bytes 14 | tf_op jit(solution)/shard_map/ppermute | solution.py:13
  17.6 4.0 %copy-start.3 = (bf16[96]{0:T(256)(128)(2,1)S(1)}, bf16[96]{0:T(256)(128)(2,1)}, u32[]{:S(2)}) copy-start(bf16[96]{0:T(256)(128)(2,1)} %param.11) | copy-start | bytes 580
  17.6 4.0 %copy-start.1 = (bf16[2,1,96,416]{3,2,1,0:T(8,128)(2,1)S(1)}, bf16[2,1,96,416]{3,2,1,0:T(8,128)(2,1)}, u32[]{:S(2)}) copy-start(bf16[2,1,96,416]{3,2,1,0:T(8,128)(2,1)} %param.7) | copy-start | bytes 479236
  18.0 18.3 %collective-permute-start.2 = (bf16[1,2,96,416]{3,0,2,1:T(2,128)(2,1)S(1)}, bf16[1,2,96,416]{3,0,2,1:T(2,128)(2,1)S(1)}, u32[]{:S(2)}, u32[]{:S(2)}) collective-permute-start(bf16[1,2,96,416]{3,0,2,1:T(2,128)(2,1)S(1)} %copy.128), channel_id=1, source_target_pairs={{28,0},{0,4},{4,8},{8,12},{12,16},{16,20},{20,24},{24,28},{29,1},{... | collective-permute-start | bytes 479240 | tf_op jit(solution)/shard_map/ppermute | solution.py:13
  19.0 17.3 %collective-permute-start.3 = (bf16[1,2,96,416]{3,0,2,1:T(2,128)(2,1)S(1)}, bf16[1,2,96,416]{3,0,2,1:T(2,128)(2,1)S(1)}, u32[]{:S(2)}, u32[]{:S(2)}) collective-permute-start(bf16[1,2,96,416]{3,0,2,1:T(2,128)(2,1)S(1)} %copy.129), channel_id=1, source_target_pairs={{4,0},{8,4},{12,8},{16,12},{20,16},{24,20},{28,24},{0,28},{5,1},{9... | collective-permute-start | bytes 479240 | tf_op jit(solution)/shard_map/ppermute | solution.py:13
  105.8 10.7 %copy-start = (bf16[27,96,384]{2,1,0:T(8,128)(2,1)S(1)}, bf16[27,96,384]{2,1,0:T(8,128)(2,1)}, u32[]{:S(2)}) copy-start(bf16[27,96,384]{2,1,0:T(8,128)(2,1)} %param.12) | copy-start | bytes 5971972
  148.9 0.7 copy-start.2
Sparse Core Ops, SparseCore 0:
  39.7 47.2 all-gather.1
where the time goes:
time: 158 us
  waiting for transfers between devices  45.3 us (29%)
  local copies, waits for them, and re-layouts  39.2 us (25%)
  other arithmetic  23.1 us (15%)
  between operations  17.7 us (11%)
  blocking collectives  12.7 us (8%)
  matrix products  11.2 us (7%)
  starting transfers between devices  8.27 us (5%)
    all_gather x1, waiting for transfers between devices, shards(): lax.all_gather(extended, 'mp', axis=2, tiled=True)  45.3 us
    another operation x2, local copies, waits for them, and re-layouts  36.1 us
    mul x1, other arithmetic, apply_taps(): shifted = padded[:, :, :, step_x:step_x + pixels + 2 * row_width] * inside  18.8 us
    psum x1, blocking collectives, shards(): squares = lax.psum(partial_squares, 'mp')  12.7 us
    dot_general x27, matrix products, apply_taps(): jnp.einsum('oc,stcp->stop', weights[step_t * 9 + step_y * 3 + step_x], wi...  8.54 us
    ppermute x4, starting transfers between devices, shifted_2(): return lax.ppermute(block, axis, route)  8.23 us
  transfers between devices with their start and end apart: 5, of which 1 were waited for; matrix products, arithmetic and copies ran while one was open for 3% of the time, Pallas kernels for 0%

commit v1 on v0

--- a/solution.py
+++ b/solution.py
@@ -5,6 +5,23 @@
 
 SECTION_CHANNELS = 384
 LATENT_COLUMNS = 104
+
+
+def laid_out(pieces, dim):
+    pieces = jnp.moveaxis(pieces, 0, dim)
+    dims = pieces.shape
+    return pieces.reshape(*dims[:dim], dims[dim] * dims[dim + 1], *dims[dim + 2 :])
+
+
+def collect(value, axis, dim):
+    size = lax.axis_size(axis)
+    right = [(i, (i + 1) % size) for i in range(size)]
+    blocks = [value]
+    while len(blocks) < size:
+        blocks.append(lax.ppermute(blocks[-1], axis, right))
+    here = lax.axis_index(axis)
+    blocks = jnp.stack(blocks)[(here - jnp.arange(size)) % size]
+    return laid_out(blocks, dim)
 
 
 def shifted_2(block, axis, distance):
@@ -99,9 +116,7 @@
     squares = lax.psum(partial_squares, "mp")
     hidden = normalize(latents, squares, norm_gain)
     extended = jnp.concatenate([moved, hidden], axis=1)
-    conv_sum = apply_taps(
-        start_zero, lax.all_gather(extended, "mp", axis=2, tiled=True), conv_weight, LATENT_COLUMNS
-    )
+    conv_sum = apply_taps(start_zero, collect(extended, "mp", 2), conv_weight, LATENT_COLUMNS)
     total = latents.astype(jnp.float32) + conv_sum + conv_bias[:, None]
     decoded = jnp.where(live, total, jnp.zeros_like(total)).astype(jnp.bfloat16)
     new_cache = extended[:, frames:]

time: 158 us -> 106 us (0.67)
  the two profiles are of different devices: /device:TPU:0 before, /device:TPU:2 now
where the time goes in v1:
time: 106 us
  waiting for transfers between devices  41.9 us (40%)
  other arithmetic  15.7 us (15%)
  local copies, waits for them, and re-layouts  13.9 us (13%)
  matrix products  12.8 us (12%)
  blocking collectives  12 us (11%)
  starting transfers between devices  5.77 us (5%)
  between operations  4.16 us (4%)
    ppermute x3, waiting for transfers between devices, collect(): blocks.append(lax.ppermute(blocks[-1], axis, right))  41.9 us
    psum x1, blocking collectives, shards(): squares = lax.psum(partial_squares, 'mp')  12 us
    dot_general x27, matrix products, apply_taps(): jnp.einsum('oc,stcp->stop', weights[step_t * 9 + step_y * 3 + step_x], wi...  10.2 us
    another operation x2, other arithmetic, collect(): blocks = jnp.stack(blocks)[(here - jnp.arange(size)) % size]  6.54 us
    gather x1, local copies, waits for them, and re-layouts, collect(): blocks = jnp.stack(blocks)[(here - jnp.arange(size)) % size]  6.28 us
    ppermute x4, starting transfers between devices, shifted_2(): return lax.ppermute(block, axis, route)  5.71 us
    mul x1, other arithmetic, apply_taps(): shifted = padded[:, :, :, step_x:step_x + pixels + 2 * row_width] * inside  5.69 us
    reshape x1, local copies, waits for them, and re-layouts, laid_out(): pieces.reshape(*dims[:dim], dims[dim] * dims[dim + 1], *dims[dim + 2:])  2.37 us
  transfers between devices with their start and end apart: 7, of which 3 were waited for; matrix products, arithmetic and copies ran while one was open for 6% of the time, Pallas kernels for 0%

profile of v1, /device:TPU:2, one launch (start us, length us, event | category | flops | bytes accessed | tf_op | source)
XLA Modules:
  0.0 106.2 jit_solution(6733355435470318716)
XLA Ops:
  0.6 0.7 fusion.116
  1.7 0.6 select_reduce_fusion.1
  2.9 1.0 collective-permute-start
  4.6 2.9 %collective-permute-start.1 = (bf16[1]{0:T(256)(128)(2,1)}, bf16[1]{0:T(256)(128)(2,1)}, u32[]{:S(2)}, u32[]{:S(2)}) collective-permute-start(bf16[1]{0:T(256)(128)(2,1)} %bitcast.7), channel_id=1, source_target_pairs={{4,0},{8,4},{12,8},{16,12},{20,16},{24,20},{28,24},{0,28},{5,1},{9... | collective-permute-start | bytes 14 | tf_op jit(solution)/shard_map/ppermute | solution.py:30
  7.5 1.4 %copy.78 = bf16[2,2,96,416]{3,0,2,1:T(2,128)(2,1)S(1)} copy(bf16[2,2,96,416]{3,2,1,0:T(8,128)(2,1)} %param.8) | data formatting | bytes 638976 | tf_op args[1]
  8.9 0.6 fusion.111
  9.9 0.6 fusion.109
  10.8 1.8 %collective-permute-start.3 = (bf16[1,2,96,416]{3,0,2,1:T(2,128)(2,1)S(1)}, bf16[1,2,96,416]{3,0,2,1:T(2,128)(2,1)S(1)}, u32[]{:S(2)}, u32[]{:S(2)}) collective-permute-start(bf16[1,2,96,416]{3,0,2,1:T(2,128)(2,1)S(1)} %copy.77), channel_id=1, source_target_pairs={{4,0},{8,4},{12,8},{16,12},{20,16},{24,20},{28,24},{0,28},{5,1},{9... | collective-permute-start | bytes 479240 | tf_op jit(solution)/shard_map/ppermute | solution.py:30
  12.6 12.0 %psum.7 = f32[2,1,1,416]{3,0,2,1:T(2,128)S(1)} all-reduce(f32[2,1,1,416]{3,0,2,1:T(2,128)S(1)} %bitcast.377), channel_id=1, replica_groups=mesh['req'=8,'mp'=4] {'mp'}, use_global_device_ids=true, to_apply=%region_3.4 | all-reduce | flops 832 | bytes 6656 | tf_op jit(solution)/shard_map/psum | solution.py:116
  26.5 1.5 %convolution_convert_fusion = bf16[2,2,96,416]{3,0,2,1:T(2,128)(2,1)S(1)} fusion(bf16[1,2,96,416]{3,0,2,1:T(2,128)(2,1)S(1)} %collective-permute-done.3, bf16[1,2,96,416]{3,0,2,1:T(2,128)(2,1)S(1)} %collective-permute-done.2, bf16[2,2,96,416]{3,0,2,1:T(2,128)(2,1)S(1)} %copy.78, f32[4]{0:T(128)S(1)} %pad_maximum_fusion.4), kind=kOutput, calls=%fused_computation.8 | convolution fusion | flops 3354632 | bytes 958480 | tf_op jit(solution)/shard_map/ns,sfkp->nfkp/dot_general | solution.py:92
  28.0 0.9 pad_maximum_fusion.3
  28.9 15.8 %collective-permute-done.4 = bf16[2,3,96,416]{3,0,2,1:T(2,128)(2,1)S(1)} collective-permute-done((bf16[2,3,96,416]{3,0,2,1:T(2,128)(2,1)S(1)}, bf16[2,3,96,416]{3,0,2,1:T(2,128)(2,1)S(1)}, u32[]{:S(2)}, u32[]{:S(2)}) %collective-permute-start.4) | collective-permute-done | bytes 479264 | tf_op jit(solution)/shard_map/ppermute | solution.py:21
  45.4 14.3 %collective-permute-done.5 = bf16[2,3,96,416]{3,0,2,1:T(2,128)(2,1)S(1)} collective-permute-done((bf16[2,3,96,416]{3,0,2,1:T(2,128)(2,1)S(1)}, bf16[2,3,96,416]{3,0,2,1:T(2,128)(2,1)S(1)}, u32[]{:S(2)}, u32[]{:S(2)}) %collective-permute-start.5) | collective-permute-done | bytes 479264 | tf_op jit(solution)/shard_map/ppermute | solution.py:21
  59.7 0.6 fusion.25
  60.3 0.8 copy.83
  61.1 0.9 fusion.124
  62.0 11.8 %collective-permute-done.6 = bf16[2,3,96,416]{3,0,2,1:T(2,128)(2,1)S(1)} collective-permute-done((bf16[2,3,96,416]{3,0,2,1:T(2,128)(2,1)S(1)}, bf16[2,3,96,416]{3,0,2,1:T(2,128)(2,1)S(1)}, u32[]{:S(2)}, u32[]{:S(2)}) %collective-permute-start.6) | collective-permute-done | bytes 479264 | tf_op jit(solution)/shard_map/ppermute | solution.py:21
  73.8 5.7 %pad_maximum_fusion = bf16[4,2,3,96,416]{4,1,3,2,0:T(2,128)(2,1)S(1)} fusion(bf16[1,2,3,96,416]{4,1,3,2,0:T(2,128)(2,1)S(1)} %bitcast.376, bf16[1,2,3,96,416]{4,1,3,2,0:T(2,128)(2,1)} %bitcast.375, bf16[1,2,3,96,416]{4,1,3,2,0:T(2,128)(2,1)S(1)} %bitcast.374, bf16[1,2,3,96,416]{4,1,3,2,0:T(2,128)(2,1)S(1)} %fusion.124), kind=kLoop, calls=%fused_computation.7 | loop fusion | flops 2875392 | bytes 3833856 | tf_op jit(solution)/shard_map/stack | solution.py:23
  79.4 6.3 %gather_fusion = bf16[4,2,3,96,416]{4,1,3,2,0:T(2,128)(2,1)} fusion(bf16[4,2,3,96,416]{4,1,3,2,0:T(2,128)(2,1)S(1)} %pad_maximum_fusion, s32[1024]{0:T(1024)S(1)} %pad_clamp_fusion), kind=kCustom, calls=%fused_computation | custom fusion | bytes 3833872 | tf_op jit(solution)/shard_map/gather | solution.py:23
  85.7 2.1 %copy.80 = bf16[2,3,4,96,416]{4,3,2,1,0:T(8,128)(2,1)S(1)} copy(bf16[2,3,4,96,416]{4,0,3,1,2:T(2,128)(2,1)} %bitcast.372) | data formatting | bytes 3833856 | tf_op jit(solution)/shard_map/transpose | solution.py:11
  87.9 2.4 %copy.81 = bf16[2,3,384,416]{2,3,0,1:T(8,128)(2,1)} copy(bf16[2,3,384,416]{3,2,1,0:T(8,128)(2,1)S(1)} %bitcast.373) | data formatting | bytes 3833856 | tf_op jit(solution)/shard_map/reshape | solution.py:13
  90.2 5.7 %fusion = (bf16[2,3,384,624]{2,3,0,1:T(8,128)(2,1)S(1)}, bf16[2,3,384,624]{2,3,0,1:T(8,128)(2,1)S(1)}, bf16[2,3,384,624]{2,3,0,1:T(8,128)(2,1)S(1)}) fusion(bf16[2,3,384,416]{2,3,0,1:T(8,128)(2,1)} %copy.81, bf16[624]{0:T(1024)(128)(2,1)S(1)} %get-tuple-element.19, bf16[624]{0:T(1024)(128)(2,1)S(1)} %fusion.105, bf16[624]{0:T(1024)(128)(2,1)S(1)} %get-tuple-element.18), kind=kLoop, calls=%fused_computation.4 | loop fusion | flops 17252352 | bytes 10546848 | tf_op jit(solution)/shard_map/mul | solution.py:42
  96.3 0.3 convolution_bitcast_fusion.1
  96.6 0.3 convolution_bitcast_fusion.2
  97.0 0.3 convolution_bitcast_fusion.3
  97.3 0.3 convolution_bitcast_fusion.4
  97.7 0.3 convolution_bitcast_fusion.5
  98.0 0.3 convolution_bitcast_fusion.6
  98.4 0.3 convolution_bitcast_fusion.7
  98.7 0.3 convolution_bitcast_fusion.8
  99.1 0.3 fusion.24
  99.4 0.3 convolution_add_fusion.14
  99.8 0.4 convolution_add_fusion.13
  100.1 0.3 convolution_add_fusion.12
  100.5 0.3 convolution_add_fusion.11
  100.8 0.3 convolution_add_fusion.10
  101.2 0.4 convolution_add_fusion.9
  101.5 0.3 convolution_add_fusion.8
  101.9 0.4 convolution_add_fusion.7
  102.2 0.3 convolution_bitcast_fusion.9
  102.6 0.4 convolution_add_fusion.6
  102.9 0.4 convolution_add_fusion.5
  103.3 0.4 convolution_add_fusion.4
  103.6 0.3 convolution_add_fusion.3
  104.0 0.3 convolution_add_fusion.2
  104.3 0.3 convolution_add_fusion.1
  104.7 0.4 fusion.3
  105.0 1.2 %fusion.20 = bf16[2,1,96,416]{3,2,1,0:T(8,128)(2,1)} fusion(f32[2,1,96,416]{3,2,0,1:T(8,128)S(1)} %convolution_bitcast_fusion, f32[2,1,96,416]{3,2,0,1:T(8,128)S(1)} %convolution_bitcast_fusion.1, f32[2,1,96,416]{3,2,0,1:T(8,128)S(1)} %convolution_bitcast_fusion.2, f32[2,1,96,416]{3,2,0,1:T(8,128)S(1)} %convolution_bitcast_fusion.3, ...), kind=kOutput, calls=%fused_computation.52 | convolution fusion | flops 62619648 | bytes 5395456 | tf_op jit(solution)/shard_map/oc,stcp->stop/dot_general | solution.py:46
  (37 shorter events, 2.1 us)
Async XLA Ops:
  2.9 22.1 %collective-permute-start = (bf16[1]{0:T(256)(128)(2,1)}, bf16[1]{0:T(256)(128)(2,1)}, u32[]{:S(2)}, u32[]{:S(2)}) collective-permute-start(bf16[1]{0:T(256)(128)(2,1)} %bitcast.4), channel_id=1, source_target_pairs={{28,0},{0,4},{4,8},{8,12},{12,16},{16,20},{20,24},{24,28},{29,1},{... | collective-permute-start | bytes 14 | tf_op jit(solution)/shard_map/ppermute | solution.py:30
  4.6 8.0 %copy-start.4 = (bf16[96]{0:T(256)(128)(2,1)S(1)}, bf16[96]{0:T(256)(128)(2,1)}, u32[]{:S(2)}) copy-start(bf16[96]{0:T(256)(128)(2,1)} %param.11) | copy-start | bytes 580
  4.6 8.0 %copy-start.1 = (bf16[2,1,96,416]{3,2,1,0:T(8,128)(2,1)S(1)}, bf16[2,1,96,416]{3,2,1,0:T(8,128)(2,1)}, u32[]{:S(2)}) copy-start(bf16[2,1,96,416]{3,2,1,0:T(8,128)(2,1)} %param.7) | copy-start | bytes 479236
  4.6 21.1 %collective-permute-start.1 = (bf16[1]{0:T(256)(128)(2,1)}, bf16[1]{0:T(256)(128)(2,1)}, u32[]{:S(2)}, u32[]{:S(2)}) collective-permute-start(bf16[1]{0:T(256)(128)(2,1)} %bitcast.7), channel_id=1, source_target_pairs={{4,0},{8,4},{12,8},{16,12},{20,16},{24,20},{28,24},{0,28},{5,1},{9... | collective-permute-start | bytes 14 | tf_op jit(solution)/shard_map/ppermute | solution.py:30
  9.8 16.7 %collective-permute-start.2 = (bf16[1,2,96,416]{3,0,2,1:T(2,128)(2,1)S(1)}, bf16[1,2,96,416]{3,0,2,1:T(2,128)(2,1)S(1)}, u32[]{:S(2)}, u32[]{:S(2)}) collective-permute-start(bf16[1,2,96,416]{3,0,2,1:T(2,128)(2,1)S(1)} %copy.76), channel_id=1, source_target_pairs={{28,0},{0,4},{4,8},{8,12},{12,16},{16,20},{20,24},{24,28},{29,1},{... | collective-permute-start | bytes 479240 | tf_op jit(solution)/shard_map/ppermute | solution.py:30
  10.8 15.7 %collective-permute-start.3 = (bf16[1,2,96,416]{3,0,2,1:T(2,128)(2,1)S(1)}, bf16[1,2,96,416]{3,0,2,1:T(2,128)(2,1)S(1)}, u32[]{:S(2)}, u32[]{:S(2)}) collective-permute-start(bf16[1,2,96,416]{3,0,2,1:T(2,128)(2,1)S(1)} %copy.77), channel_id=1, source_target_pairs={{4,0},{8,4},{12,8},{16,12},{20,16},{24,20},{28,24},{0,28},{5,1},{9... | collective-permute-start | bytes 479240 | tf_op jit(solution)/shard_map/ppermute | solution.py:30
  28.8 15.9 %collective-permute-start.4 = (bf16[2,3,96,416]{3,0,2,1:T(2,128)(2,1)S(1)}, bf16[2,3,96,416]{3,0,2,1:T(2,128)(2,1)S(1)}, u32[]{:S(2)}, u32[]{:S(2)}) collective-permute-start(bf16[2,3,96,416]{3,0,2,1:T(2,128)(2,1)S(1)} %pad_maximum_fusion.3), channel_id=1, source_target_pairs={{0,1},{1,2},{2,3},{3,0},{4,5},{5,6},{6,7},{7,4},{8,9},{9,10},{10,1... | collective-permute-start | bytes 1437704 | tf_op jit(solution)/shard_map/ppermute | solution.py:21
  44.7 15.0 %collective-permute-start.5 = (bf16[2,3,96,416]{3,0,2,1:T(2,128)(2,1)S(1)}, bf16[2,3,96,416]{3,0,2,1:T(2,128)(2,1)S(1)}, u32[]{:S(2)}, u32[]{:S(2)}) collective-permute-start(bf16[2,3,96,416]{3,0,2,1:T(2,128)(2,1)S(1)} %collective-permute-done.4), channel_id=1, source_target_pairs={{0,1},{1,2},{2,3},{3,0},{4,5},{5,6},{6,7},{7,4},{8,9},{9,10},{10,1... | collective-permute-start | bytes 1437704 | tf_op jit(solution)/shard_map/ppermute | solution.py:21
  59.6 14.1 %copy-start.2 = (bf16[2,3,96,416]{3,0,2,1:T(2,128)(2,1)}, bf16[2,3,96,416]{3,0,2,1:T(2,128)(2,1)S(1)}, u32[]{:S(2)}) copy-start(bf16[2,3,96,416]{3,0,2,1:T(2,128)(2,1)S(1)} %collective-permute-done.5) | copy-start | bytes 1437700
  59.7 14.1 %collective-permute-start.6 = (bf16[2,3,96,416]{3,0,2,1:T(2,128)(2,1)S(1)}, bf16[2,3,96,416]{3,0,2,1:T(2,128)(2,1)S(1)}, u32[]{:S(2)}, u32[]{:S(2)}) collective-permute-start(bf16[2,3,96,416]{3,0,2,1:T(2,128)(2,1)S(1)} %collective-permute-done.5), channel_id=1, source_target_pairs={{0,1},{1,2},{2,3},{3,0},{4,5},{5,6},{6,7},{7,4},{8,9},{9,10},{10,1... | collective-permute-start | bytes 1437704 | tf_op jit(solution)/shard_map/ppermute | solution.py:21
  90.2 5.7 %copy-start = (bf16[27,96,384]{2,1,0:T(8,128)(2,1)S(1)}, bf16[27,96,384]{2,1,0:T(8,128)(2,1)}, u32[]{:S(2)}) copy-start(bf16[27,96,384]{2,1,0:T(8,128)(2,1)} %param.12) | copy-start | bytes 5971972
  103.6 1.4 %copy-start.3 = (f32[96]{0:T(128)S(1)}, f32[96]{0:T(128)}, u32[]{:S(2)}) copy-start(f32[96]{0:T(128)} %param.13) | copy-start | bytes 1156
